TPU v7x, 32 devices: a whole 2x2x4 slice. The times are simulated.
32 devices in a mesh: expert: 16 (over z, y, x), replica: 2 (over core).
Axes of the slice: x: 2, y: 2, z: 4, core: 2. Of those that a mesh axis runs over, the one named last changes fastest.
Arguments:
- tokens: bfloat16 [1024, 7168], P('expert', 'replica'), may hold values from -6 to 6
- routes: int32 [1024, 8], P('expert'), may hold values from 0 to 15, all different within a row; in each aligned block of 64 rows (0 to 63, 64 to 127, ...) at most 64 rows name the same one
- route_scores: float32 [1024, 8], P('expert'), may hold values from 0.05 to 1
- placement: int32 [16], replicated, may hold values from 0 to 15, each once
- w_in: bfloat16 [16, 7168, 2, 1024], P('expert', 'replica'), may hold values from -0.0625 to 0.0625
- w_out: bfloat16 [16, 1024, 7168], P('expert', None, 'replica'), may hold values from -0.1875 to 0.1875
Outputs:
- mixed: bfloat16 [1024, 7168], P('expert', 'replica')
Inputs may be any that keep to these rules, and one draw needn't show every extreme that they name: `routes`: each row names 8 different logical experts. Among the 64 rows of each aligned block (the tokens of one index of the expert axis) no expert is named by more than 64 rows, a bound that some block reaches. `placement`: A permutation of the physical slots.
All inputs are finite; a program needn't handle non-finite values.
Results may differ from a plain program's by a relative error of at most 0.0057.
Values may be sent and summed in bfloat16 or wider, within the bound.
A program may use at most 128 MiB of HBM per device.

v0:
```python
import jax
import jax.numpy as jnp
from jax import lax
from jax.sharding import PartitionSpec as P


def on_device(tokens, routes, route_scores, placement, w_in, w_out):
    tok_rows, feature_cols = tokens.shape
    route_count = routes.shape[1]
    experts = placement.shape[0]
    hidden_units = w_in.shape[3]
    capacity = min(tok_rows, max(2, 2 * tok_rows * route_count // experts))
    slot_total = experts * capacity
    expert_ids = jnp.arange(experts, dtype=jnp.int32)
    route_table = routes[:, :, None] == expert_ids
    physical = jnp.sum(jnp.where(route_table, placement, 0), axis=-1)
    flat_slots = physical.reshape(-1)
    onehot = (flat_slots[:, None] == expert_ids).astype(jnp.int32)
    earlier = jnp.sum((jnp.cumsum(onehot, axis=0) - onehot) * onehot, axis=1)
    position = (flat_slots * capacity + earlier).reshape(tok_rows, route_count)
    slot_index = jnp.arange(slot_total, dtype=jnp.int32)
    placing = jnp.any(position[None, :, :] == slot_index[:, None, None], axis=-1).astype(
        jnp.bfloat16
    )
    outgoing = jnp.dot(placing, tokens, preferred_element_type=jnp.float32).astype(jnp.bfloat16)
    incoming = lax.all_to_all(outgoing, "expert", split_axis=0, concat_axis=0, tiled=True)
    weights_in = w_in[0].reshape(feature_cols, 2 * hidden_units)
    weights_out = w_out[0]
    partial_value = jnp.dot(incoming, weights_in, preferred_element_type=jnp.float32)
    partial_value = partial_value.reshape(slot_total, 2, hidden_units)
    shares = lax.psum_scatter(partial_value, "replica", scatter_dimension=2, tiled=True)
    active = (jax.nn.silu(shares[:, 0]) * shares[:, 1]).astype(jnp.bfloat16)
    result = jnp.dot(
        lax.all_gather(active, "replica", axis=1, tiled=True),
        weights_out,
        preferred_element_type=jnp.float32,
    )
    expert_out = result.astype(jnp.bfloat16)
    returned = lax.all_to_all(expert_out, "expert", split_axis=0, concat_axis=0, tiled=True)
    route_weight = 2.5 * route_scores / jnp.sum(route_scores, axis=1, keepdims=True)
    picked = returned[position.reshape(-1)].reshape(tok_rows, route_count, feature_cols)
    mixed = jnp.sum(picked.astype(jnp.float32) * route_weight[:, :, None], axis=1)
    return mixed.astype(jnp.bfloat16)


def solution(mesh):
    in_specs = (
        P("expert", "replica"),
        P("expert", None),
        P("expert", None),
        P(),
        P("expert", "replica", None, None),
        P("expert", None, "replica"),
    )
    out_specs = P("expert", "replica")
    return jax.shard_map(
        on_device, mesh=mesh, in_specs=in_specs, out_specs=out_specs, check_vma=False
    )
```

profile of v0, /device:TPU:28, one launch (start us, length us, event | category | flops | bytes accessed | tf_op | source)
XLA Modules:
  0.0 454.1 jit_solution(2317390866444530714)
XLA Ops:
  6.5 0.8 select_reduce_fusion
  7.5 0.1 eq.58
  7.6 0.1 eq.54
  7.7 1.2 reduce-window.6
  8.8 0.2 slice_reduce_fusion
  9.1 0.1 fusion.7
  9.2 0.1 reduce_sum.42
  9.3 0.1 copy.18
  9.4 0.7 fusion.4
  10.2 5.1 %convolution_convert_fusion.1 = bf16[1024,3584]{1,0:T(8,128)(2,1)} fusion(pred[1024,64]{0,1:T(8,128)(4,1)S(1)} %fusion.4, bf16[64,3584]{1,0:T(8,128)(2,1)S(1)} %copy-done), kind=kOutput, calls=%fused_computation.2 | convolution fusion | flops 473432064 | bytes 7864320 | tf_op jit(solution)/shard_map/dot_general | solution.py:25
  15.3 7.0 %all-to-all-start = ((bf16[16,64,3584]{2,1,0:T(8,128)(2,1)}), bf16[16,64,3584]{2,1,0:T(8,128)(2,1)}, u32[]{:S(2)}, u32[]{:S(2)}) async-start(bf16[16,64,3584]{2,1,0:T(8,128)(2,1)} %bitcast.55), calls=%async_computation | async-start | bytes 14680064 | tf_op jit(solution)/shard_map/all_to_all | solution.py:26
  22.3 16.0 %copy.23 = bf16[448,8,2,1024]{3,1,2,0:T(8,128)(2,1)} copy(bf16[448,8,2,1024]{3,2,1,0:T(2,128)(2,1)} %bitcast.56) | data formatting | bytes 29360128
  38.3 18.8 %copy.19 = bf16[2048,3584]{1,0:T(8,128)(2,1)} copy(bf16[2048,3584]{0,1:T(8,128)(2,1)} %bitcast.54) | data formatting | bytes 29360128 | tf_op jit(solution)/shard_map/dot_general | solution.py:29
  57.1 131.5 %all-to-all-done = bf16[16,64,3584]{2,1,0:T(8,128)(2,1)} async-done(((bf16[16,64,3584]{2,1,0:T(8,128)(2,1)}), bf16[16,64,3584]{2,1,0:T(8,128)(2,1)}, u32[]{:S(2)}, u32[]{:S(2)}) %all-to-all-start) | async-done | bytes 7340064 | tf_op jit(solution)/shard_map/all_to_all | solution.py:26
  188.6 21.6 %fusion.10 = f32[1024,2,1024]{2,0,1:T(8,128)} fusion(bf16[1024,3584,1]{1,0,2:T(8,128)(2,1)} %bitcast.3, bf16[2,1024,3584]{2,1,0:T(8,128)(2,1)} %bitcast.57), kind=kOutput, calls=%fused_computation.28 | convolution fusion | flops 15032385536 | bytes 30408704 | tf_op jit(solution)/shard_map/dot_general | solution.py:29
  210.2 16.7 %reduce-scatter.2.cloned.1.call-done = f32[1024,2,512]{2,0,1:T(8,128)} async-done(((f32[1024,2,1024]{2,0,1:T(8,128)}), f32[1024,2,512]{2,0,1:T(8,128)}) %reduce-scatter.2.cloned.1.call-update) | async-done | bytes 4194320 | tf_op jit(solution)/shard_map/reduce_scatter | solution.py:31
  226.9 3.8 fusion.3
  230.8 11.9 %all-gather.2.cloned.1.call-done = bf16[1024,1024]{1,0:T(8,128)(2,1)} async-done(((bf16[1024,512]{1,0:T(8,128)(2,1)}), bf16[1024,1024]{1,0:T(8,128)(2,1)}) %all-gather.2.cloned.1.call-update) | async-done | bytes 2097168 | tf_op jit(solution)/shard_map/all_gather | solution.py:34
  242.7 12.5 %convolution_convert_fusion = bf16[1024,3584]{1,0:T(8,128)(2,1)} fusion(bf16[1024,1024]{1,0:T(8,128)(2,1)} %all-gather.2.cloned.1.call-done, bf16[1,1024,3584]{2,1,0:T(8,128)(2,1)} %param.11), kind=kOutput, calls=%fused_computation.1 | convolution fusion | flops 7519862784 | bytes 16777216 | tf_op jit(solution)/shard_map/dot_general | solution.py:33
  255.2 7.1 %all-to-all-start.1 = ((bf16[16,64,3584]{2,1,0:T(8,128)(2,1)}), bf16[16,64,3584]{2,1,0:T(8,128)(2,1)}, u32[]{:S(2)}, u32[]{:S(2)}) async-start(bf16[16,64,3584]{2,1,0:T(8,128)(2,1)} %bitcast.58), calls=%async_computation.2 | async-start | bytes 14680064 | tf_op jit(solution)/shard_map/all_to_all | solution.py:39
  262.4 0.1 mul.49
  262.6 166.8 %all-to-all-done.1 = bf16[16,64,3584]{2,1,0:T(8,128)(2,1)} async-done(((bf16[16,64,3584]{2,1,0:T(8,128)(2,1)}), bf16[16,64,3584]{2,1,0:T(8,128)(2,1)}, u32[]{:S(2)}, u32[]{:S(2)}) %all-to-all-start.1) | async-done | bytes 7340064 | tf_op jit(solution)/shard_map/all_to_all | solution.py:39
  429.4 12.0 %gather_fusion = bf16[512,3584]{1,0:T(8,128)(2,1)} fusion(bf16[1024,3584]{1,0:T(8,128)(2,1)} %bitcast.10, s32[1024]{0:T(1024)S(1)} %pad_clamp_fusion), kind=kCustom, calls=%fused_computation | custom fusion | bytes 7342080 | tf_op jit(solution)/shard_map/gather | solution.py:41
  441.4 5.8 %fusion = bf16[64,3584]{1,0:T(8,128)(2,1)} fusion(bf16[512,3584]{1,0:T(8,128)(2,1)} %gather_fusion, f32[64,8]{1,0:T(8,128)S(1)} %copy.21), kind=kLoop, calls=%fused_computation.4 | loop fusion | flops 5275648 | bytes 4130816 | tf_op jit(solution)/shard_map/reduce_sum | solution.py:42
  (22 shorter events, 0.5 us)
Async XLA Ops:
  6.5 3.6 copy-start
  15.3 173.3 %all-to-all-start = ((bf16[16,64,3584]{2,1,0:T(8,128)(2,1)}), bf16[16,64,3584]{2,1,0:T(8,128)(2,1)}, u32[]{:S(2)}, u32[]{:S(2)}) async-start(bf16[16,64,3584]{2,1,0:T(8,128)(2,1)} %bitcast.55), calls=%async_computation | async-start | bytes 14680064 | tf_op jit(solution)/shard_map/all_to_all | solution.py:26
  22.2 204.7 %reduce-scatter.2.cloned.1.call-start = ((), (), s32[]{:S(2)}) async-start(), calls=%async_computation.3 | async-start | bytes 12582912 | tf_op jit(solution)/shard_map/reduce_scatter | solution.py:31
  210.2 32.5 %all-gather.2.cloned.1.call-start = ((), (), s32[]{:S(2)}) async-start(), calls=%async_computation.4 | async-start | bytes 3145728 | tf_op jit(solution)/shard_map/all_gather | solution.py:34
  255.2 7.2 %copy-start.2 = (f32[64,8]{0,1:T(8,128)S(1)}, f32[64,8]{0,1:T(8,128)}, u32[]{:S(2)}) copy-start(f32[64,8]{0,1:T(8,128)} %param.8) | copy-start | bytes 6148
  255.2 174.2 %all-to-all-start.1 = ((bf16[16,64,3584]{2,1,0:T(8,128)(2,1)}), bf16[16,64,3584]{2,1,0:T(8,128)(2,1)}, u32[]{:S(2)}, u32[]{:S(2)}) async-start(bf16[16,64,3584]{2,1,0:T(8,128)(2,1)} %bitcast.58), calls=%async_computation.2 | async-start | bytes 14680064 | tf_op jit(solution)/shard_map/all_to_all | solution.py:39
  429.4 17.8 %copy-start.1 = (bf16[64,3584]{1,0:T(8,128)(2,1)S(1)}, bf16[64,3584]{1,0:T(8,128)(2,1)}, u32[]{:S(2)}) copy-start(bf16[64,3584]{1,0:T(8,128)(2,1)} %param.6) | copy-start | bytes 1376260
Sparse Core Ops, SparseCore 0:
  210.3 16.5 reduce-scatter.1
  230.9 11.7 all-gather.1
where the time goes:
time: 455 us; the launch traced here: 454 us
  waiting for transfers between devices  327 us (72%)
  local copies, waits for them, and re-layouts  47.8 us (11%)
  matrix products  39.3 us (9%)
  starting transfers between devices  14.1 us (3%)
  between operations  13.5 us (3%)
  other arithmetic  12.6 us (3%)
    all_to_all x1, waiting for transfers between devices, on_device(): lax.all_to_all(expert_out, 'expert', split_axis=0, concat_axis=0, tiled=T...  167 us
    all_to_all x1, waiting for transfers between devices, on_device(): lax.all_to_all(outgoing, 'expert', split_axis=0, concat_axis=0, tiled=True)  131 us
    dot_general x1, matrix products, on_device(): jnp.dot(incoming, weights_in, preferred_element_type=jnp.float32)  21.6 us
    dot_general x1, local copies, waits for them, and re-layouts, on_device(): jnp.dot(incoming, weights_in, preferred_element_type=jnp.float32)  18.8 us
    reduce_scatter x1, waiting for transfers between devices, on_device(): lax.psum_scatter(partial_value, 'replica', scatter_dimension=2, tiled=True)  16.7 us
    unnamed x7, local copies, waits for them, and re-layouts  16 us
    dot_general x1, matrix products, on_device(): jnp.dot(lax.all_gather(active, 'replica', axis=1, tiled=True), weights_ou...  12.5 us
    gather x1, local copies, waits for them, and re-layouts, on_device(): returned[position.reshape(-1)].reshape(tok_rows, route_count, feature_cols)  12 us
  transfers between devices with their start and end apart: 4, of which 4 were waited for; matrix products, arithmetic and copies ran while one was open for 8% of the time, Pallas kernels for 0%

commit v1 on v0

--- a/solution.py
+++ b/solution.py
@@ -2,6 +2,18 @@
 import jax.numpy as jnp
 from jax import lax
 from jax.sharding import PartitionSpec as P
+
+
+def rotated_exchange(shard, axis, split, join):
+    ways, here = (lax.axis_size(axis), lax.axis_index(axis))
+    width = shard.shape[split] // ways
+    turned = jnp.roll(shard, -here * width, axis=split)
+    got = [lax.slice_in_dim(turned, 0, width, axis=split)]
+    for far in range(1, ways):
+        sent = lax.slice_in_dim(turned, far * width, (far + 1) * width, axis=split)
+        got.append(lax.ppermute(sent, axis, [(d, (d + far) % ways) for d in range(ways)]))
+    line = jnp.concatenate(got[::-1], axis=join)
+    return jnp.roll(line, (here + 1) * got[0].shape[join], axis=join)
 
 
 def on_device(tokens, routes, route_scores, placement, w_in, w_out):
@@ -36,7 +48,7 @@
         preferred_element_type=jnp.float32,
     )
     expert_out = result.astype(jnp.bfloat16)
-    returned = lax.all_to_all(expert_out, "expert", split_axis=0, concat_axis=0, tiled=True)
+    returned = rotated_exchange(expert_out, "expert", 0, 0)
     route_weight = 2.5 * route_scores / jnp.sum(route_scores, axis=1, keepdims=True)
     picked = returned[position.reshape(-1)].reshape(tok_rows, route_count, feature_cols)
     mixed = jnp.sum(picked.astype(jnp.float32) * route_weight[:, :, None], axis=1)

time: 455 us -> 526 us (1.16)
  the two profiles are of different devices: /device:TPU:28 before, /device:TPU:8 now
where the time goes in v1:
time: 526 us; the launch traced here: 525 us
  waiting for transfers between devices  302 us (57%)
  local copies, waits for them, and re-layouts  67.1 us (13%)
  starting transfers between devices  65.5 us (12%)
  matrix products  39.2 us (7%)
  other arithmetic  37.6 us (7%)
  between operations  13.5 us (3%)
    ppermute x15, waiting for transfers between devices, rotated_exchange(): lax.ppermute(sent, axis, [(d, (d + far) % ways) for d in range(ways)])  143 us
    all_to_all x1, waiting for transfers between devices, on_device(): lax.all_to_all(outgoing, 'expert', split_axis=0, concat_axis=0, tiled=True)  123 us
    ppermute x15, starting transfers between devices, rotated_exchange(): lax.ppermute(sent, axis, [(d, (d + far) % ways) for d in range(ways)])  58 us
    unnamed x22, local copies, waits for them, and re-layouts  28.2 us
    reduce_scatter x1, waiting for transfers between devices, on_device(): lax.psum_scatter(partial_value, 'replica', scatter_dimension=2, tiled=True)  24.6 us
    dot_general x1, matrix products, on_device(): jnp.dot(incoming, weights_in, preferred_element_type=jnp.float32)  21.6 us
    dot_general x1, local copies, waits for them, and re-layouts, on_device(): jnp.dot(incoming, weights_in, preferred_element_type=jnp.float32)  18.7 us
    concatenate x1, other arithmetic, rotated_exchange(): turned = jnp.roll(shard, -here * width, axis=split)  12.5 us
  transfers between devices with their start and end apart: 18, of which 15 were waited for; matrix products, arithmetic and copies ran while one was open for 9% of the time, Pallas kernels for 0%

profile of v1, /device:TPU:8, one launch (start us, length us, event | category | flops | bytes accessed | tf_op | source)
XLA Modules:
  0.0 525.2 jit_solution(9416930360163315893)
XLA Ops:
  10.2 5.1 convolution_convert_fusion.1
  15.3 7.2 %all-to-all-start = ((bf16[16,64,3584]{2,1,0:T(8,128)(2,1)}), bf16[16,64,3584]{2,1,0:T(8,128)(2,1)}, u32[]{:S(2)}, u32[]{:S(2)}) async-start(bf16[16,64,3584]{2,1,0:T(8,128)(2,1)} %bitcast.53), calls=%async_computation | async-start | bytes 14680064 | tf_op jit(solution)/shard_map/all_to_all | solution.py:38
  22.5 16.0 %copy.23 = bf16[448,8,2,1024]{3,1,2,0:T(8,128)(2,1)} copy(bf16[448,8,2,1024]{3,2,1,0:T(2,128)(2,1)} %bitcast.54) | data formatting | bytes 29360128
  38.6 18.7 %copy.19 = bf16[2048,3584]{1,0:T(8,128)(2,1)} copy(bf16[2048,3584]{0,1:T(8,128)(2,1)} %bitcast.52) | data formatting | bytes 29360128 | tf_op jit(solution)/shard_map/dot_general | solution.py:41
  57.3 123.4 %all-to-all-done = bf16[16,64,3584]{2,1,0:T(8,128)(2,1)} async-done(((bf16[16,64,3584]{2,1,0:T(8,128)(2,1)}), bf16[16,64,3584]{2,1,0:T(8,128)(2,1)}, u32[]{:S(2)}, u32[]{:S(2)}) %all-to-all-start) | async-done | bytes 7340064 | tf_op jit(solution)/shard_map/all_to_all | solution.py:38
  180.8 21.6 %fusion.13 = f32[1024,2,1024]{2,0,1:T(8,128)} fusion(bf16[1024,3584,1]{1,0,2:T(8,128)(2,1)} %bitcast.3, bf16[2,1024,3584]{2,1,0:T(8,128)(2,1)} %bitcast.55), kind=kOutput, calls=%fused_computation.51 | convolution fusion | flops 15032385536 | bytes 30408704 | tf_op jit(solution)/shard_map/dot_general | solution.py:41
  202.6 24.6 %reduce-scatter.2.cloned.1.call-done = f32[1024,2,512]{2,0,1:T(8,128)} async-done(((f32[1024,2,1024]{2,0,1:T(8,128)}), f32[1024,2,512]{2,0,1:T(8,128)}) %reduce-scatter.2.cloned.1.call-update) | async-done | bytes 4194320 | tf_op jit(solution)/shard_map/reduce_scatter | solution.py:43
  231.3 11.7 %all-gather.2.cloned.1.call-done = bf16[1024,1024]{1,0:T(8,128)(2,1)} async-done(((bf16[1024,512]{1,0:T(8,128)(2,1)}), bf16[1024,1024]{1,0:T(8,128)(2,1)}) %all-gather.2.cloned.1.call-update) | async-done | bytes 2097168 | tf_op jit(solution)/shard_map/all_gather | solution.py:46
  242.9 12.5 %convolution_convert_fusion = bf16[1024,3584]{1,0:T(8,128)(2,1)} fusion(bf16[1024,1024]{1,0:T(8,128)(2,1)} %all-gather.2.cloned.1.call-done, bf16[1,1024,3584]{2,1,0:T(8,128)(2,1)} %param.13), kind=kOutput, calls=%fused_computation.5 | convolution fusion | flops 7519862784 | bytes 16777216 | tf_op jit(solution)/shard_map/dot_general | solution.py:45
  255.4 12.5 %fusion.1 = bf16[1024,3584]{1,0:T(8,128)(2,1)} fusion(s32[]{:T(128)S(6)} %select_n.29, bf16[1024,3584]{1,0:T(8,128)(2,1)} %convolution_convert_fusion), kind=kLoop, calls=%fused_computation.8 | loop fusion | flops 14680064 | bytes 14680068 | tf_op jit(solution)/shard_map/jit(_roll_dynamic)/concatenate | solution.py:10
  281.5 11.0 %collective-permute-done = bf16[64,3584]{1,0:T(8,128)(2,1)S(1)} collective-permute-done((bf16[64,3584]{1,0:T(8,128)(2,1)}, bf16[64,3584]{1,0:T(8,128)(2,1)S(1)}, u32[]{:S(2)}, u32[]{:S(2)}) %collective-permute-start) | collective-permute-done | bytes 458784 | tf_op jit(solution)/shard_map/ppermute | solution.py:14
  292.5 5.8 %collective-permute-start.5 = (bf16[64,3584]{1,0:T(8,128)(2,1)}, bf16[64,3584]{1,0:T(8,128)(2,1)S(1)}, u32[]{:S(2)}, u32[]{:S(2)}) collective-permute-start(bf16[64,3584]{1,0:T(8,128)(2,1)} %get-tuple-element.15), channel_id=1, source_target_pairs={{0,20},{2,22},{4,24},{6,26},{8,28},{10,30},{12,0},{14,2},{16,4},{1... | collective-permute-start | bytes 1376264 | tf_op jit(solution)/shard_map/ppermute | solution.py:14
  299.1 9.3 %collective-permute-done.1 = bf16[64,3584]{1,0:T(8,128)(2,1)S(1)} collective-permute-done((bf16[64,3584]{1,0:T(8,128)(2,1)}, bf16[64,3584]{1,0:T(8,128)(2,1)S(1)}, u32[]{:S(2)}, u32[]{:S(2)}) %collective-permute-start.1) | collective-permute-done | bytes 458784 | tf_op jit(solution)/shard_map/ppermute | solution.py:14
  309.1 9.0 %collective-permute-done.2 = bf16[64,3584]{1,0:T(8,128)(2,1)S(1)} collective-permute-done((bf16[64,3584]{1,0:T(8,128)(2,1)}, bf16[64,3584]{1,0:T(8,128)(2,1)S(1)}, u32[]{:S(2)}, u32[]{:S(2)}) %collective-permute-start.2) | collective-permute-done | bytes 458784 | tf_op jit(solution)/shard_map/ppermute | solution.py:14
  321.3 8.8 %collective-permute-done.3 = bf16[64,3584]{1,0:T(8,128)(2,1)S(1)} collective-permute-done((bf16[64,3584]{1,0:T(8,128)(2,1)}, bf16[64,3584]{1,0:T(8,128)(2,1)S(1)}, u32[]{:S(2)}, u32[]{:S(2)}) %collective-permute-start.3) | collective-permute-done | bytes 458784 | tf_op jit(solution)/shard_map/ppermute | solution.py:14
  331.0 27.9 %collective-permute-done.4 = bf16[64,3584]{1,0:T(8,128)(2,1)S(1)} collective-permute-done((bf16[64,3584]{1,0:T(8,128)(2,1)}, bf16[64,3584]{1,0:T(8,128)(2,1)S(1)}, u32[]{:S(2)}, u32[]{:S(2)}) %collective-permute-start.4) | collective-permute-done | bytes 458784 | tf_op jit(solution)/shard_map/ppermute | solution.py:14
  359.8 35.1 %collective-permute-done.5 = bf16[64,3584]{1,0:T(8,128)(2,1)S(1)} collective-permute-done((bf16[64,3584]{1,0:T(8,128)(2,1)}, bf16[64,3584]{1,0:T(8,128)(2,1)S(1)}, u32[]{:S(2)}, u32[]{:S(2)}) %collective-permute-start.5) | collective-permute-done | bytes 458784 | tf_op jit(solution)/shard_map/ppermute | solution.py:14
  395.7 9.9 %collective-permute-done.6 = bf16[64,3584]{1,0:T(8,128)(2,1)S(1)} collective-permute-done((bf16[64,3584]{1,0:T(8,128)(2,1)}, bf16[64,3584]{1,0:T(8,128)(2,1)S(1)}, u32[]{:S(2)}, u32[]{:S(2)}) %collective-permute-start.6) | collective-permute-done | bytes 458784 | tf_op jit(solution)/shard_map/ppermute | solution.py:14
  405.6 36.6 %collective-permute-start.11 = (bf16[64,3584]{1,0:T(8,128)(2,1)S(1)}, bf16[64,3584]{1,0:T(8,128)(2,1)S(1)}, u32[]{:S(2)}, u32[]{:S(2)}) collective-permute-start(bf16[64,3584]{1,0:T(8,128)(2,1)S(1)} %get-tuple-element.9), channel_id=1, source_target_pairs={{0,8},{2,10},{4,12},{6,14},{8,16},{10,18},{12,20},{14,22},{16,24},... | collective-permute-start | bytes 1376264 | tf_op jit(solution)/shard_map/ppermute | solution.py:14
  460.1 8.9 %collective-permute-done.11 = bf16[64,3584]{1,0:T(8,128)(2,1)S(1)} collective-permute-done((bf16[64,3584]{1,0:T(8,128)(2,1)S(1)}, bf16[64,3584]{1,0:T(8,128)(2,1)S(1)}, u32[]{:S(2)}, u32[]{:S(2)}) %collective-permute-start.11) | collective-permute-done | bytes 458784 | tf_op jit(solution)/shard_map/ppermute | solution.py:14
  474.9 10.3 %collective-permute-done.14 = bf16[64,3584]{1,0:T(8,128)(2,1)S(1)} collective-permute-done((bf16[64,3584]{1,0:T(8,128)(2,1)S(1)}, bf16[64,3584]{1,0:T(8,128)(2,1)S(1)}, u32[]{:S(2)}, u32[]{:S(2)}) %collective-permute-start.14) | collective-permute-done | bytes 458784 | tf_op jit(solution)/shard_map/ppermute | solution.py:14
  487.8 12.5 %fusion = bf16[1024,3584]{1,0:T(8,128)(2,1)} fusion(s32[]{:T(128)S(6)} %select_n.31, bf16[1024,3584]{1,0:T(8,128)(2,1)} %slice_dynamic-update-slice_fusion), kind=kLoop, calls=%fused_computation.7 | loop fusion | flops 14680064 | bytes 14680068 | tf_op jit(solution)/shard_map/jit(_roll_dynamic)/concatenate | solution.py:16
  500.3 12.3 %gather_fusion = bf16[512,3584]{1,0:T(8,128)(2,1)} fusion(bf16[1024,3584]{1,0:T(8,128)(2,1)} %fusion, s32[1024]{0:T(1024)S(1)} %pad_clamp_fusion), kind=kCustom, calls=%fused_computation | custom fusion | bytes 7342080 | tf_op jit(solution)/shard_map/gather | solution.py:53
  512.6 5.8 %fusion.2 = bf16[64,3584]{1,0:T(8,128)(2,1)} fusion(bf16[512,3584]{1,0:T(8,128)(2,1)} %gather_fusion, f32[64,8]{1,0:T(8,128)S(1)} %copy.21), kind=kLoop, calls=%fused_computation.10 | loop fusion | flops 5275648 | bytes 4130816 | tf_op jit(solution)/shard_map/reduce_sum | solution.py:54
  (69 shorter events, 55.0 us)
Async XLA Ops:
  6.5 3.6 copy-start
  15.3 165.5 %all-to-all-start = ((bf16[16,64,3584]{2,1,0:T(8,128)(2,1)}), bf16[16,64,3584]{2,1,0:T(8,128)(2,1)}, u32[]{:S(2)}, u32[]{:S(2)}) async-start(bf16[16,64,3584]{2,1,0:T(8,128)(2,1)} %bitcast.53), calls=%async_computation | async-start | bytes 14680064 | tf_op jit(solution)/shard_map/all_to_all | solution.py:38
  22.5 204.7 %reduce-scatter.2.cloned.1.call-start = ((), (), s32[]{:S(2)}) async-start(), calls=%async_computation.2 | async-start | bytes 12582912 | tf_op jit(solution)/shard_map/reduce_scatter | solution.py:43
  202.4 28.9 %copy-start.2 = (f32[64,8]{0,1:T(8,128)S(1)}, f32[64,8]{0,1:T(8,128)}, u32[]{:S(2)}) copy-start(f32[64,8]{0,1:T(8,128)} %param.10) | copy-start | bytes 6148
  202.4 40.6 %all-gather.2.cloned.1.call-start = ((), (), s32[]{:S(2)}) async-start(), calls=%async_computation.3 | async-start | bytes 3145728 | tf_op jit(solution)/shard_map/all_gather | solution.py:46
  273.1 19.4 %collective-permute-start = (bf16[64,3584]{1,0:T(8,128)(2,1)}, bf16[64,3584]{1,0:T(8,128)(2,1)S(1)}, u32[]{:S(2)}, u32[]{:S(2)}) collective-permute-start(bf16[64,3584]{1,0:T(8,128)(2,1)} %get-tuple-element.20), channel_id=1, source_target_pairs={{0,30},{2,0},{4,2},{6,4},{8,6},{10,8},{12,10},{14,12},{16,14},{18,... | collective-permute-start | bytes 1376264 | tf_op jit(solution)/shard_map/ppermute | solution.py:14
  275.5 32.8 %collective-permute-start.1 = (bf16[64,3584]{1,0:T(8,128)(2,1)}, bf16[64,3584]{1,0:T(8,128)(2,1)S(1)}, u32[]{:S(2)}, u32[]{:S(2)}) collective-permute-start(bf16[64,3584]{1,0:T(8,128)(2,1)} %get-tuple-element.19), channel_id=1, source_target_pairs={{0,28},{2,30},{4,0},{6,2},{8,4},{10,6},{12,8},{14,10},{16,12},{18,... | collective-permute-start | bytes 1376264 | tf_op jit(solution)/shard_map/ppermute | solution.py:14
  276.0 42.2 %collective-permute-start.2 = (bf16[64,3584]{1,0:T(8,128)(2,1)}, bf16[64,3584]{1,0:T(8,128)(2,1)S(1)}, u32[]{:S(2)}, u32[]{:S(2)}) collective-permute-start(bf16[64,3584]{1,0:T(8,128)(2,1)} %get-tuple-element.18), channel_id=1, source_target_pairs={{0,26},{2,28},{4,30},{6,0},{8,2},{10,4},{12,6},{14,8},{16,10},{18,... | collective-permute-start | bytes 1376264 | tf_op jit(solution)/shard_map/ppermute | solution.py:14
  279.5 50.7 %collective-permute-start.3 = (bf16[64,3584]{1,0:T(8,128)(2,1)}, bf16[64,3584]{1,0:T(8,128)(2,1)S(1)}, u32[]{:S(2)}, u32[]{:S(2)}) collective-permute-start(bf16[64,3584]{1,0:T(8,128)(2,1)} %get-tuple-element.17), channel_id=1, source_target_pairs={{0,24},{2,26},{4,28},{6,30},{8,0},{10,2},{12,4},{14,6},{16,8},{18,... | collective-permute-start | bytes 1376264 | tf_op jit(solution)/shard_map/ppermute | solution.py:14
  280.0 78.9 %collective-permute-start.4 = (bf16[64,3584]{1,0:T(8,128)(2,1)}, bf16[64,3584]{1,0:T(8,128)(2,1)S(1)}, u32[]{:S(2)}, u32[]{:S(2)}) collective-permute-start(bf16[64,3584]{1,0:T(8,128)(2,1)} %get-tuple-element.16), channel_id=1, source_target_pairs={{0,22},{2,24},{4,26},{6,28},{8,30},{10,0},{12,2},{14,4},{16,6},{18... | collective-permute-start | bytes 1376264 | tf_op jit(solution)/shard_map/ppermute | solution.py:14
  292.5 102.4 %collective-permute-start.5 = (bf16[64,3584]{1,0:T(8,128)(2,1)}, bf16[64,3584]{1,0:T(8,128)(2,1)S(1)}, u32[]{:S(2)}, u32[]{:S(2)}) collective-permute-start(bf16[64,3584]{1,0:T(8,128)(2,1)} %get-tuple-element.15), channel_id=1, source_target_pairs={{0,20},{2,22},{4,24},{6,26},{8,28},{10,30},{12,0},{14,2},{16,4},{1... | collective-permute-start | bytes 1376264 | tf_op jit(solution)/shard_map/ppermute | solution.py:14
  308.3 97.3 %collective-permute-start.6 = (bf16[64,3584]{1,0:T(8,128)(2,1)}, bf16[64,3584]{1,0:T(8,128)(2,1)S(1)}, u32[]{:S(2)}, u32[]{:S(2)}) collective-permute-start(bf16[64,3584]{1,0:T(8,128)(2,1)} %get-tuple-element.14), channel_id=1, source_target_pairs={{0,18},{2,20},{4,22},{6,24},{8,26},{10,28},{12,30},{14,0},{16,2},{... | collective-permute-start | bytes 1376264 | tf_op jit(solution)/shard_map/ppermute | solution.py:14
  318.1 124.9 %collective-permute-start.7 = (bf16[64,3584]{1,0:T(8,128)(2,1)}, bf16[64,3584]{1,0:T(8,128)(2,1)S(1)}, u32[]{:S(2)}, u32[]{:S(2)}) collective-permute-start(bf16[64,3584]{1,0:T(8,128)(2,1)} %get-tuple-element.13), channel_id=1, source_target_pairs={{0,16},{2,18},{4,20},{6,22},{8,24},{10,26},{12,28},{14,30},{16,0},... | collective-permute-start | bytes 1376264 | tf_op jit(solution)/shard_map/ppermute | solution.py:14
  330.1 113.7 %collective-permute-start.8 = (bf16[64,3584]{1,0:T(8,128)(2,1)}, bf16[64,3584]{1,0:T(8,128)(2,1)S(1)}, u32[]{:S(2)}, u32[]{:S(2)}) collective-permute-start(bf16[64,3584]{1,0:T(8,128)(2,1)} %get-tuple-element.12), channel_id=1, source_target_pairs={{0,14},{2,16},{4,18},{6,20},{8,22},{10,24},{12,26},{14,28},{16,30}... | collective-permute-start | bytes 1376264 | tf_op jit(solution)/shard_map/ppermute | solution.py:14
  358.9 90.6 %collective-permute-start.9 = (bf16[64,3584]{1,0:T(8,128)(2,1)}, bf16[64,3584]{1,0:T(8,128)(2,1)S(1)}, u32[]{:S(2)}, u32[]{:S(2)}) collective-permute-start(bf16[64,3584]{1,0:T(8,128)(2,1)} %get-tuple-element.11), channel_id=1, source_target_pairs={{0,12},{2,14},{4,16},{6,18},{8,20},{10,22},{12,24},{14,26},{16,28}... | collective-permute-start | bytes 1376264 | tf_op jit(solution)/shard_map/ppermute | solution.py:14
  394.9 64.4 %collective-permute-start.10 = (bf16[64,3584]{1,0:T(8,128)(2,1)S(1)}, bf16[64,3584]{1,0:T(8,128)(2,1)S(1)}, u32[]{:S(2)}, u32[]{:S(2)}) collective-permute-start(bf16[64,3584]{1,0:T(8,128)(2,1)S(1)} %get-tuple-element.10), channel_id=1, source_target_pairs={{0,10},{2,12},{4,14},{6,16},{8,18},{10,20},{12,22},{14,24},{16,26}... | collective-permute-start | bytes 1376264 | tf_op jit(solution)/shard_map/ppermute | solution.py:14
  405.6 63.4 %collective-permute-start.11 = (bf16[64,3584]{1,0:T(8,128)(2,1)S(1)}, bf16[64,3584]{1,0:T(8,128)(2,1)S(1)}, u32[]{:S(2)}, u32[]{:S(2)}) collective-permute-start(bf16[64,3584]{1,0:T(8,128)(2,1)S(1)} %get-tuple-element.9), channel_id=1, source_target_pairs={{0,8},{2,10},{4,12},{6,14},{8,16},{10,18},{12,20},{14,22},{16,24},... | collective-permute-start | bytes 1376264 | tf_op jit(solution)/shard_map/ppermute | solution.py:14
  443.0 26.8 %collective-permute-start.12 = (bf16[64,3584]{1,0:T(8,128)(2,1)S(1)}, bf16[64,3584]{1,0:T(8,128)(2,1)S(1)}, u32[]{:S(2)}, u32[]{:S(2)}) collective-permute-start(bf16[64,3584]{1,0:T(8,128)(2,1)S(1)} %get-tuple-element.8), channel_id=1, source_target_pairs={{0,6},{2,8},{4,10},{6,12},{8,14},{10,16},{12,18},{14,20},{16,22},{... | collective-permute-start | bytes 1376264 | tf_op jit(solution)/shard_map/ppermute | solution.py:14
  443.9 30.2 %collective-permute-start.13 = (bf16[64,3584]{1,0:T(8,128)(2,1)S(1)}, bf16[64,3584]{1,0:T(8,128)(2,1)S(1)}, u32[]{:S(2)}, u32[]{:S(2)}) collective-permute-start(bf16[64,3584]{1,0:T(8,128)(2,1)S(1)} %get-tuple-element.7), channel_id=1, source_target_pairs={{0,4},{2,6},{4,8},{6,10},{8,12},{10,14},{12,16},{14,18},{16,20},{1... | collective-permute-start | bytes 1376264 | tf_op jit(solution)/shard_map/ppermute | solution.py:14
  449.5 35.7 %collective-permute-start.14 = (bf16[64,3584]{1,0:T(8,128)(2,1)S(1)}, bf16[64,3584]{1,0:T(8,128)(2,1)S(1)}, u32[]{:S(2)}, u32[]{:S(2)}) collective-permute-start(bf16[64,3584]{1,0:T(8,128)(2,1)S(1)} %get-tuple-element.6), channel_id=1, source_target_pairs={{0,2},{2,4},{4,6},{6,8},{8,10},{10,12},{12,14},{14,16},{16,18},{18... | collective-permute-start | bytes 1376264 | tf_op jit(solution)/shard_map/ppermute | solution.py:14
  500.3 18.1 %copy-start.1 = (bf16[64,3584]{1,0:T(8,128)(2,1)S(1)}, bf16[64,3584]{1,0:T(8,128)(2,1)}, u32[]{:S(2)}) copy-start(bf16[64,3584]{1,0:T(8,128)(2,1)} %param.8) | copy-start | bytes 1376260
Sparse Core Ops, SparseCore 0:
  202.5 24.6 reduce-scatter.1
  231.1 11.7 all-gather.1
